TPU v7x, 256 devices: a whole 4x4x8 slice. The times are simulated.
256 devices in a mesh: panel: 16 (over z, y_hi), mic: 8 (over x, core), tm: 2 (over y_lo).
Axes of the slice: x: 4, y: 4 (y_hi: 2, y_lo: 2; y = y_hi * 2 + y_lo), z: 8, core: 2. Of those that a mesh axis runs over, the one named last changes fastest.
Arguments:
- sources: bfloat16 [16384, 8, 256], P('panel', None, 'tm'), may hold values from -6 to 6
- transfer_matrix: bfloat16 [4096, 16384], P('mic', 'panel'), may hold values from -0.046875 to 0.046875
- delay_groups: int32 [128, 32], P('panel', 'mic'), may hold values from 0 to 32
- patch_block: int32 [128], P('panel'), may hold values from 0 to 127, as said below
Outputs:
- normal_product: bfloat16 [16384, 8, 256], P(('panel', 'mic'), None, 'tm')
Inputs may be any that keep to these rules, and one draw needn't show every extreme that they name: No two patches share a value, and patch q's value lies in the same run of 8 blocks as q itself (q // 8 == patch_block[q] // 8).
All inputs are finite; a program needn't handle non-finite values.
Results may differ from a plain program's by a relative error of at most 0.017.
Values may be sent and summed in bfloat16 or wider, within the bound.
A program may use at most 64 MiB of HBM per device.

v0:
```python
import jax
import jax.numpy as jnp
from jax import lax
from jax.sharding import PartitionSpec as P

DMAX = 32
PATCH = 128
MB = 128


def from_behind(value, axis, steps):
    count = lax.axis_size(axis)
    initial, last = (max(0, -steps), min(count, count - steps))
    return lax.ppermute(value, axis, [(source, source + steps) for source in range(initial, last)])


def shift_slabs(slabs, offsets, length):

    def one_slab(single_slab, offset_value):
        return lax.dynamic_slice_in_dim(single_slab, offset_value, length, axis=2)

    return jax.vmap(one_slab)(slabs, offsets)


def per_device(sources, transfer_matrix, delay_groups, patch_block):
    panel_dev, nvec, half = sources.shape
    mic_dev = transfer_matrix.shape[0]
    patch_dev = panel_dev // PATCH
    mic_blocks = mic_dev // MB
    local_block = patch_block - lax.axis_index("panel") * patch_dev
    rim = from_behind(sources[:, :, half - DMAX :], "tm", 1)
    extended = jnp.concatenate([rim, sources], axis=2)
    in_patches = extended.reshape(patch_dev, PATCH, nvec, half + DMAX)[local_block]
    partials = []
    for mic_block in range(mic_blocks):
        shifted = shift_slabs(in_patches, DMAX - delay_groups[:, mic_block], half)
        shifted = shifted.reshape(panel_dev, nvec, half)
        weights = transfer_matrix[mic_block * MB : (mic_block + 1) * MB]
        partials.append(
            jnp.einsum("mp,pnt->mnt", weights, shifted, preferred_element_type=jnp.float32)
        )
    partial_value = jnp.concatenate(partials, axis=0)
    pressure = lax.psum(partial_value, "panel").astype(jnp.bfloat16)
    tail = from_behind(pressure[:, :, :DMAX], "tm", -1)
    padded = jnp.concatenate([pressure, tail], axis=2)
    patch_ids = jnp.arange(patch_dev, dtype=jnp.int32)
    owner_patch = jnp.sum(
        jnp.where(local_block[None, :] == patch_ids[:, None], patch_ids[None, :], 0), axis=1
    )
    tiles = transfer_matrix.reshape(mic_dev, patch_dev, PATCH)
    row_count = panel_dev // lax.axis_size("mic") * lax.axis_size("mic")
    patch_count = row_count // PATCH
    chosen_tiles = tiles[:, owner_patch]
    chosen_delays = delay_groups[owner_patch]
    accum = jnp.zeros((patch_count, PATCH, nvec, half), jnp.float32)
    for mic_block in range(mic_blocks):
        rows = padded[mic_block * MB : (mic_block + 1) * MB]

        def advance(offset_value):
            return lax.dynamic_slice_in_dim(rows, offset_value, half, axis=2)

        advanced = jax.vmap(advance)(chosen_delays[:, mic_block])
        block_tiles = chosen_tiles[mic_block * MB : (mic_block + 1) * MB]
        accum = accum + jnp.einsum(
            "mqp,qmnt->qpnt", block_tiles, advanced, preferred_element_type=jnp.float32
        )
    return lax.psum_scatter(
        accum.reshape(row_count, nvec, half).astype(jnp.bfloat16),
        "mic",
        scatter_dimension=0,
        tiled=True,
    )


def solution(mesh):
    placed = (P("panel", None, "tm"), P("mic", "panel"), P("panel", "mic"), P("panel"))
    return jax.shard_map(
        per_device,
        mesh=mesh,
        in_specs=placed,
        out_specs=P(("panel", "mic"), None, "tm"),
        check_vma=False,
    )
```

profile of v0, /device:TPU:16, one launch (start us, length us, event | category | flops | bytes accessed | tf_op | source)
XLA Modules:
  0.0 273.3 jit_solution(14391907746548980314)
XLA Ops:
  10.2 3.2 %collective-permute-start = (bf16[1024,8,32]{0,2,1:T(8,128)(2,1)S(1)}, bf16[1024,8,32]{0,2,1:T(8,128)(2,1)S(1)}, u32[]{:S(2)}, u32[]{:S(2)}) collective-permute-start(bf16[1024,8,32]{0,2,1:T(8,128)(2,1)S(1)} %copy.171), channel_id=1, source_target_pairs={{0,1},{2,3},{4,5},{6,7},{8,9},{10,11},{12,13},{14,15},{16,17},{18,... | collective-permute-start | bytes 1572872 | tf_op jit(solution)/shard_map/ppermute | solution.py:14
  14.0 10.6 %collective-permute-done = bf16[1024,8,32]{0,2,1:T(8,128)(2,1)S(1)} collective-permute-done((bf16[1024,8,32]{0,2,1:T(8,128)(2,1)S(1)}, bf16[1024,8,32]{0,2,1:T(8,128)(2,1)S(1)}, u32[]{:S(2)}, u32[]{:S(2)}) %collective-permute-start) | collective-permute-done | bytes 524320 | tf_op jit(solution)/shard_map/ppermute | solution.py:14
  26.2 5.2 %pad_maximum_fusion = bf16[1024,8,160]{2,1,0:T(8,128)(2,1)} fusion(bf16[1024,8,128]{2,1,0:T(8,128)(2,1)} %param.4, bf16[1024,8,32]{2,1,0:T(8,128)(2,1)S(1)} %copy.130), kind=kLoop, calls=%fused_computation.11 | loop fusion | flops 5242880 | bytes 5242880 | tf_op jit(solution)/shard_map/concatenate | solution.py:32
  31.4 6.8 %copy.132 = bf16[8,128,8,160]{1,3,2,0:T(8,128)(2,1)S(1)} copy(bf16[8,128,8,160]{3,2,1,0:T(8,128)(2,1)} %bitcast.58) | data formatting | bytes 5242880 | tf_op jit(solution)/shard_map/reshape | solution.py:33
  38.2 2.4 gather_fusion.1
  40.6 2.8 %copy.134 = bf16[8,128,8,160]{1,2,0,3:T(8,128)(2,1)S(1)} copy(bf16[8,128,8,160]{1,3,2,0:T(8,128)(2,1)} %gather_fusion.1) | data formatting | bytes 5242880 | tf_op jit(solution)/shard_map/gather | solution.py:33
  43.4 2.5 gather_fusion.10
  45.9 4.1 %copy.170 = bf16[8,128,8,128]{3,1,0,2:T(8,128)(2,1)} copy(bf16[8,128,8,128]{1,2,3,0:T(8,128)(2,1)} %gather_fusion.10) | data formatting | bytes 4194304 | tf_op jit(solution)/shard_map/reshape | solution.py:37
  50.0 2.5 gather_fusion.9
  52.6 4.1 %copy.169 = bf16[8,128,8,128]{3,1,0,2:T(8,128)(2,1)} copy(bf16[8,128,8,128]{1,2,3,0:T(8,128)(2,1)} %gather_fusion.9) | data formatting | bytes 4194304 | tf_op jit(solution)/shard_map/reshape | solution.py:37
  56.7 3.1 %convolution_bitcast_fusion = f32[128,8,128]{2,0,1:T(8,128)} fusion(bf16[1024,8,128]{2,0,1:T(8,128)(2,1)} %bitcast.61, bf16[512,1024]{1,0:T(8,128)(2,1)} %param.5), kind=kOutput, calls=%fused_computation.27 | convolution fusion | flops 268435456 | bytes 2883584 | tf_op jit(solution)/shard_map/mp,pnt->mnt/dot_general | solution.py:40
  62.0 2.6 gather_fusion.8
  64.6 2.5 gather_fusion.7
  67.1 4.2 %copy.167 = bf16[8,128,8,128]{3,1,0,2:T(8,128)(2,1)} copy(bf16[8,128,8,128]{1,2,3,0:T(8,128)(2,1)} %gather_fusion.7) | data formatting | bytes 4194304 | tf_op jit(solution)/shard_map/reshape | solution.py:37
  71.3 3.0 %convolution_bitcast_fusion.3 = f32[128,8,128]{2,0,1:T(8,128)} fusion(bf16[1024,8,128]{2,0,1:T(8,128)(2,1)} %bitcast.63, bf16[512,1024]{1,0:T(8,128)(2,1)S(1)} %copy-done.2), kind=kOutput, calls=%fused_computation.30 | convolution fusion | flops 268435456 | bytes 2883584 | tf_op jit(solution)/shard_map/mp,pnt->mnt/dot_general | solution.py:40
  74.3 2.9 %copy.168 = bf16[8,128,8,128]{3,1,0,2:T(8,128)(2,1)} copy(bf16[8,128,8,128]{1,2,3,0:T(8,128)(2,1)S(1)} %copy-done) | data formatting | bytes 4194304 | tf_op jit(solution)/shard_map/reshape | solution.py:37
  79.5 110.6 %all-reduce.9 = bf16[512,8,128]{2,0,1:T(8,128)(2,1)S(1)} all-reduce(f32[512,8,128]{2,0,1:T(8,128)S(1)} %pad_maximum_fusion.1), channel_id=1, replica_groups=mesh['panel'=16,'mic'=8,'tm'=2] {'panel'}, use_global_device_ids=true, to_apply=%region_1.2 | all-reduce | flops 524288 | bytes 3145728 | tf_op jit(solution)/shard_map/psum | solution.py:43
  197.9 2.7 collective-permute-done.1
  208.8 4.3 %fusion.5 = f32[8,128,8,128]{3,1,2,0:T(8,128)} fusion(bf16[8,128,8,128]{1,2,3,0:T(8,128)(2,1)} %gather_fusion.3, bf16[512,8,128]{0,2,1:T(8,128)(2,1)} %bitcast.65), kind=kOutput, calls=%fused_computation.25 | convolution fusion | flops 268435456 | bytes 6553600 | tf_op jit(solution)/shard_map/mqp,qmnt->qpnt/dot_general | solution.py:64
  213.1 3.6 %fusion.3 = f32[8,128,8,128]{3,1,2,0:T(8,128)} fusion(bf16[8,128,8,128]{1,2,3,0:T(8,128)(2,1)S(1)} %gather_fusion.4, bf16[512,8,128]{0,2,1:T(8,128)(2,1)} %bitcast.66), kind=kOutput, calls=%fused_computation.23 | convolution fusion | flops 268435456 | bytes 6553600 | tf_op jit(solution)/shard_map/mqp,qmnt->qpnt/dot_general | solution.py:64
  217.7 3.6 %fusion.1 = f32[8,128,8,128]{3,1,2,0:T(8,128)} fusion(bf16[8,128,8,128]{1,2,3,0:T(8,128)(2,1)S(1)} %gather_fusion.5, bf16[512,8,128]{0,2,1:T(8,128)(2,1)} %bitcast.67), kind=kOutput, calls=%fused_computation.21 | convolution fusion | flops 268435456 | bytes 6553600 | tf_op jit(solution)/shard_map/mqp,qmnt->qpnt/dot_general | solution.py:64
  222.3 5.8 %add_convert_fusion = bf16[8,128,8,128]{3,1,2,0:T(8,128)(2,1)S(1)} fusion(f32[8,128,8,128]{3,1,2,0:T(8,128)} %fusion.1, f32[8,128,8,128]{3,1,2,0:T(8,128)} %fusion.5, f32[8,128,8,128]{3,1,2,0:T(8,128)} %fusion.3, bf16[8,128,8,128]{1,2,3,0:T(8,128)(2,1)S(1)} %gather_fusion.6, bf16[512,8,128]{0,2,1:T(8,128)(2,1)} %bitcast.68), kind=kOutput, calls=%fused_computation.12 | convolution fusion | flops 272629760 | bytes 17039360 | tf_op jit(solution)/shard_map/mqp,qmnt->qpnt/dot_general | solution.py:64
  228.2 2.8 %copy.160 = bf16[8,128,8,128]{3,2,1,0:T(8,128)(2,1)} copy(bf16[8,128,8,128]{3,1,2,0:T(8,128)(2,1)S(1)} %add_convert_fusion) | data formatting | bytes 4194304 | tf_op jit(solution)/shard_map/convert_element_type | solution.py:68
  231.0 35.5 %reduce-scatter.2.cloned.1.call-done = bf16[128,8,128]{2,1,0:T(8,128)(2,1)} async-done(((bf16[1024,8,128]{2,1,0:T(8,128)(2,1)}), bf16[128,8,128]{2,1,0:T(8,128)(2,1)}) %reduce-scatter.2.cloned.1.call-update) | async-done | bytes 262160 | tf_op jit(solution)/shard_map/reduce_scatter | solution.py:67
  (50 shorter events, 28.1 us)
Async XLA Ops:
  6.5 259.9 %reduce-scatter.2.cloned.1.call-start = ((), (), s32[]{:S(2)}) async-start(), calls=%async_computation.1 | async-start | bytes 2359296 | tf_op jit(solution)/shard_map/reduce_scatter | solution.py:67
  8.8 4.7 %copy-start.7 = (s32[8]{0:T(128)S(1)}, s32[8]{0:T(128)}, u32[]{:S(2)}) copy-start(s32[8]{0:T(128)} %param.7) | copy-start | bytes 100
  8.8 4.9 %copy-start.6 = (s32[8,4]{0,1:T(4,128)S(1)}, s32[8,4]{0,1:T(4,128)}, u32[]{:S(2)}) copy-start(s32[8,4]{0,1:T(4,128)} %param.6) | copy-start | bytes 388
  10.2 14.4 %collective-permute-start = (bf16[1024,8,32]{0,2,1:T(8,128)(2,1)S(1)}, bf16[1024,8,32]{0,2,1:T(8,128)(2,1)S(1)}, u32[]{:S(2)}, u32[]{:S(2)}) collective-permute-start(bf16[1024,8,32]{0,2,1:T(8,128)(2,1)S(1)} %copy.171), channel_id=1, source_target_pairs={{0,1},{2,3},{4,5},{6,7},{8,9},{10,11},{12,13},{14,15},{16,17},{18,... | collective-permute-start | bytes 1572872 | tf_op jit(solution)/shard_map/ppermute | solution.py:14
  56.7 3.1 %copy-start.1 = (bf16[8,128,8,128]{3,1,0,2:T(8,128)(2,1)S(1)}, bf16[8,128,8,128]{3,1,0,2:T(8,128)(2,1)}, u32[]{:S(2)}) copy-start(bf16[8,128,8,128]{3,1,0,2:T(8,128)(2,1)} %copy.169) | copy-start | bytes 6291460
  67.1 4.2 %copy-start.2 = (bf16[512,1024]{1,0:T(8,128)(2,1)S(1)}, bf16[512,1024]{1,0:T(8,128)(2,1)}, u32[]{:S(2)}) copy-start(bf16[512,1024]{1,0:T(8,128)(2,1)} %param.5) | copy-start | bytes 3145732
  71.3 3.0 %copy-start = (bf16[8,128,8,128]{1,2,3,0:T(8,128)(2,1)S(1)}, bf16[8,128,8,128]{1,2,3,0:T(8,128)(2,1)}, u32[]{:S(2)}) copy-start(bf16[8,128,8,128]{1,2,3,0:T(8,128)(2,1)} %gather_fusion.8) | copy-start | bytes 6291460
  77.2 2.2 copy-start.3
  77.2 2.2 copy-start.4
  77.2 2.2 copy-start.5
  191.2 9.4 %collective-permute-start.1 = (bf16[512,8,32]{0,2,1:T(8,128)(2,1)}, bf16[512,8,32]{0,2,1:T(8,128)(2,1)S(1)}, u32[]{:S(2)}, u32[]{:S(2)}) collective-permute-start(bf16[512,8,32]{0,2,1:T(8,128)(2,1)} %copy.149), channel_id=1, source_target_pairs={{1,0},{3,2},{5,4},{7,6},{9,8},{11,10},{13,12},{15,14},{17,16},{19,... | collective-permute-start | bytes 786440 | tf_op jit(solution)/shard_map/ppermute | solution.py:14
Sparse Core Ops, SparseCore 0:
  231.1 35.2 reduce-scatter.1
where the time goes:
time: 274 us; the launch traced here: 273 us
  blocking collectives  111 us (41%)
  local copies, waits for them, and re-layouts  60.1 us (22%)
  waiting for transfers between devices  48.8 us (18%)
  matrix products  27.9 us (10%)
  between operations  13.6 us (5%)
  other arithmetic  7.58 us (3%)
  starting transfers between devices  4.68 us (2%)
    psum x1, blocking collectives, per_device(): pressure = lax.psum(partial_value, 'panel').astype(jnp.bfloat16)  111 us
    reduce_scatter x1, waiting for transfers between devices, per_device(): lax.psum_scatter(accum.reshape(row_count, nvec, half).astype(jnp.bfloat16...  35.5 us
    dot_general x4, matrix products, per_device(): jnp.einsum('mqp,qmnt->qpnt', block_tiles, advanced, preferred_element_typ...  17.4 us
    reshape x4, local copies, waits for them, and re-layouts, per_device(): shifted = shifted.reshape(panel_dev, nvec, half)  15.3 us
    ppermute x2, waiting for transfers between devices, from_behind(): lax.ppermute(value, axis, [(source, source + steps) for source in range(i...  13.3 us
    dot_general x4, matrix products, per_device(): jnp.einsum('mp,pnt->mnt', weights, shifted, preferred_element_type=jnp.fl...  10.4 us
    gather x4, local copies, waits for them, and re-layouts, one_slab(): return lax.dynamic_slice_in_dim(single_slab, offset_value, length, axis=2)  10.2 us
    reshape x1, local copies, waits for them, and re-layouts, per_device(): extended.reshape(patch_dev, PATCH, nvec, half + DMAX)[local_block]  6.81 us
  transfers between devices with their start and end apart: 3, of which 3 were waited for; matrix products, arithmetic and copies ran while one was open for 2% of the time, Pallas kernels for 0%

commit v1 on v0

v1 whole, which is shorter than its diff:
```python
import jax
import jax.numpy as jnp
from jax import lax
from jax.experimental import pallas as pl
from jax.experimental.pallas import tpu as pltpu
from jax.sharding import PartitionSpec as P

DMAX = 32
PATCH = 128
MB = 128
NVEC = 8
NZ = 8
NX = 4
CH = 32
ROWS = CH // NZ
HALF = ROWS // 2
MESH = pl.DeviceIdType.MESH
F32 = jnp.float32
BF16 = jnp.bfloat16


def reorder(dg_ref, pb_ref, mat, delays, tiles):
    patches, blocks = dg_ref.shape
    base = lax.axis_index("panel") * patches
    for j in range(patches):
        owner = jnp.int32(0)
        for q in range(patches):
            owner = owner + jnp.where(pb_ref[q] - base == j, q, 0)
        for b in range(blocks):
            delays[j * blocks + b] = dg_ref[owner, b]
        cols = pl.ds(pl.multiple_of(owner * PATCH, PATCH), PATCH)
        tiles[:, j * PATCH : (j + 1) * PATCH] = mat[:, cols]


def body(
    delays, src_hbm, mat_hbm, out_ref,
    sbuf, tiles, fa, fb, st, part, rs_recv, rs_send, y_send, y_recv, o_recv, gath, work,
    g_send, g_keep, g_recv, x0_send, x0_recv, x1_send, x1_recv, fin,
    in_sem, rs_ss, rs_rs, y_ss, y_rs, o_ss, o_rs, ag_ss, ag_rs, c_ss, c_rs, x0_ss, x0_rs, x1_ss, x1_rs,
):
    panel_dev, nvec, half = sbuf.shape
    patches = panel_dev // PATCH
    blocks = tiles.shape[0] // MB
    panel, mic, tm = (lax.axis_index(name) for name in ("panel", "mic", "tm"))
    z, y_hi = panel // 2, panel % 2
    x, core = mic // 2, mic % 2

    def z_at(step):
        return (z + step + NZ) % NZ

    def x_at(step):
        return (x + step + NX) % NX

    def z_peer(sign):
        return {"panel": z_at(sign) * 2 + y_hi}

    def x_peer(sign):
        return {"mic": x_at(sign) * 2 + core}

    y_peer = {"panel": z * 2 + 1 - y_hi}
    o_peers = ({"tm": 1 - tm}, {"panel": z * 2 + 1 - y_hi, "tm": 1 - tm})
    core_peer = {"mic": x * 2 + 1 - core}
    signs = (1, -1)

    barrier = pltpu.get_barrier_semaphore()
    peers = [z_peer(1), z_peer(-1), y_peer, *o_peers, core_peer, x_peer(1), x_peer(-1)]
    for peer in peers:
        pl.semaphore_signal(barrier, inc=1, device_id=peer, device_id_type=MESH)

    def load_src(j):
        return pltpu.make_async_copy(
            src_hbm.at[pl.ds(j * PATCH, PATCH)], sbuf.at[pl.ds(j * PATCH, PATCH)], in_sem.at[j]
        )

    load_mat = pltpu.make_async_copy(mat_hbm, tiles, in_sem.at[patches])
    for j in range(patches):
        load_src(j).start()
    load_mat.start()

    st[0:CH] = jnp.zeros((CH,) + st.shape[1:], st.dtype)
    st[half + CH : half + 2 * CH] = jnp.zeros((CH,) + st.shape[1:], st.dtype)
    work[half : half + CH] = jnp.zeros((CH,) + work.shape[1:], work.dtype)

    @pl.loop(0, patches)
    def _(j):
        load_src(j).wait()
        fa[...] = sbuf[pl.ds(j * PATCH, PATCH)].astype(F32).reshape(PATCH * nvec, half)
        for n in range(nvec):
            fb[pl.ds(n, half, stride=nvec), :] = fa[pl.ds(n, PATCH, stride=nvec), :].T
        st[CH : CH + half, :, pl.ds(pl.multiple_of(j * PATCH, PATCH), PATCH)] = (
            fb[...].reshape(half, nvec, PATCH).astype(st.dtype)
        )

    load_mat.wait()

    pl.semaphore_wait(barrier, len(peers))

    count = jnp.where(tm == 0, 5, 4)

    def chunk_of(p):
        return jnp.where(tm == 0, 4 - p, p)

    def out_chunk(q):
        return jnp.where(tm == 0, 3 - q, q)

    def cut(way):
        return pl.ds(way * HALF, HALF)

    def rs_copy(way, step, p):
        if step == 0:
            source = part.at[chunk_of(p), z_at(4), cut(way)]
            target = rs_recv.at[way, 0, p, cut(way)]
        else:
            source = rs_send.at[way, step - 1, p]
            target = rs_recv.at[way, step, p]
        return pltpu.make_async_remote_copy(
            src_ref=source, dst_ref=target, send_sem=rs_ss.at[way, step, p], recv_sem=rs_rs.at[way, step, p],
            device_id=z_peer(signs[way]), device_id_type=MESH,
        )

    def y_copy(p):
        return pltpu.make_async_remote_copy(
            src_ref=y_send.at[p], dst_ref=y_recv.at[p], send_sem=y_ss.at[p], recv_sem=y_rs.at[p],
            device_id=y_peer, device_id_type=MESH,
        )

    def o_copy(which):
        return pltpu.make_async_remote_copy(
            src_ref=y_send.at[0], dst_ref=o_recv.at[which], send_sem=o_ss.at[which], recv_sem=o_rs.at[which],
            device_id=o_peers[which], device_id_type=MESH,
        )

    def ag_copy(way, step, p):
        owner = z_at(-signs[way] * step)
        ref = gath.at[p, owner, cut(way)] if step == 3 else gath.at[p, owner]
        return pltpu.make_async_remote_copy(
            src_ref=ref, dst_ref=ref, send_sem=ag_ss.at[way, step, p], recv_sem=ag_rs.at[way, step, p],
            device_id=z_peer(signs[way]), device_id_type=MESH,
        )

    def core_copy(q):
        return pltpu.make_async_remote_copy(
            src_ref=g_send.at[q], dst_ref=g_recv.at[q], send_sem=c_ss.at[q], recv_sem=c_rs.at[q],
            device_id=core_peer, device_id_type=MESH,
        )

    def x0_copy(way, q):
        return pltpu.make_async_remote_copy(
            src_ref=x0_send.at[way, q], dst_ref=x0_recv.at[way, q], send_sem=x0_ss.at[way, q],
            recv_sem=x0_rs.at[way, q], device_id=x_peer(signs[way]), device_id_type=MESH,
        )

    def x1_copy(way, q):
        return pltpu.make_async_remote_copy(
            src_ref=x1_send.at[way, q], dst_ref=x1_recv.at[way, q], send_sem=x1_ss.at[way, q],
            recv_sem=x1_rs.at[way, q], device_id=x_peer(signs[way]), device_id_type=MESH,
        )

    def forward(p):
        c = chunk_of(p)
        for b in range(blocks):
            pieces = []
            for j in range(patches):
                rows = pl.ds(CH * c + CH - delays[j * blocks + b], CH)
                pieces.append(st[rows, :, j * PATCH : (j + 1) * PATCH].reshape(CH * nvec, PATCH))
            acc = lax.dot_general(
                jnp.concatenate(pieces, axis=1), tiles[b * MB : (b + 1) * MB, :],
                (((1,), (1,)), ((), ())), preferred_element_type=F32,
            )
            part[c, :, :, :, b * MB : (b + 1) * MB] = acc.reshape(NZ, ROWS, nvec, MB).astype(BF16)
        for way in range(2):
            rs_copy(way, 0, p).start()

    def reduce_step(step, p):
        c = chunk_of(p)
        for way in range(2):
            rs_copy(way, step - 1, p).wait_recv()
            dest = z_at(signs[way] * (4 - step))
            if step == 1:
                here, there = cut(way), cut(1 - way)
                rs_send[way, 0, p, here] = (
                    part[c, dest, here].astype(F32) + rs_recv[way, 0, p, here].astype(F32)
                ).astype(BF16)
                rs_send[way, 0, p, there] = part[c, dest, there]
            else:
                rs_send[way, step - 1, p] = (
                    part[c, dest].astype(F32) + rs_recv[way, step - 1, p].astype(F32)
                ).astype(BF16)
            rs_copy(way, step, p).start()

    def own_sum(p):
        return (
            part[chunk_of(p), z].astype(F32) + rs_recv[0, 3, p].astype(F32) + rs_recv[1, 3, p].astype(F32)
        )

    def reduce_last(p):
        for way in range(2):
            rs_copy(way, 3, p).wait_recv()
        y_send[p] = own_sum(p).astype(BF16)
        y_copy(p).start()

        @pl.when(p == 0)
        def _():
            for which in range(2):
                o_copy(which).start()

    def gather_first(p):
        y_copy(p).wait_recv()
        total = own_sum(p) + y_recv[p].astype(F32)

        @pl.when(p == 0)
        def _():
            for which in range(2):
                o_copy(which).wait_recv()
            gath[p, z] = (total + o_recv[0].astype(F32) + o_recv[1].astype(F32)).astype(BF16)

        @pl.when(p != 0)
        def _():
            gath[p, z] = total.astype(BF16)

        for way in range(2):
            ag_copy(way, 0, p).start()

    def gather_step(step, p):
        for way in range(2):
            ag_copy(way, step - 1, p).wait_recv()
            ag_copy(way, step, p).start()

    def gather_last(p):
        for way in range(2):
            ag_copy(way, 3, p).wait_recv()
        work[pl.ds(chunk_of(p) * CH, CH)] = gath[p].reshape(CH, nvec, blocks * MB)

    def backward(q):
        start = out_chunk(q) * CH
        for target, side in ((g_send, 1 - core), (g_keep, core)):

            @pl.loop(0, NX)
            def _(k):
                j = 2 * k + side
                pieces = []
                for b in range(blocks):
                    rows = pl.ds(start + delays[j * blocks + b], CH)
                    pieces.append(work[rows, :, b * MB : (b + 1) * MB].reshape(CH * nvec, MB))
                acc = jnp.dot(
                    jnp.concatenate(pieces, axis=1), tiles[:, pl.ds(pl.multiple_of(j * PATCH, PATCH), PATCH)],
                    preferred_element_type=F32,
                )
                target[q, k] = acc.reshape(CH, nvec, PATCH).astype(BF16)

            if target is g_send:
                core_copy(q).start()

    hx = CH // 2

    def pair(q, dest, rows):
        return g_keep[q, dest, rows].astype(F32) + g_recv[q, dest, rows].astype(F32)

    def scatter_first(q):
        core_copy(q).wait_recv()
        for way in range(2):
            x0_send[way, q] = pair(q, x_at(2), pl.ds(way * hx, hx)).astype(BF16)
            x0_copy(way, q).start()

    def scatter_second(q):
        for way in range(2):
            x0_copy(way, q).wait_recv()
            dest = x_at(signs[way])
            here, there = pl.ds(way * hx, hx), pl.ds((1 - way) * hx, hx)
            x1_send[way, q, here] = (pair(q, dest, here) + x0_recv[way, q].astype(F32)).astype(BF16)
            x1_send[way, q, there] = pair(q, dest, there).astype(BF16)
            x1_copy(way, q).start()

    def scatter_last(q):
        for way in range(2):
            x1_copy(way, q).wait_recv()
        total = pair(q, x, pl.ds(0, CH)) + x1_recv[0, q].astype(F32) + x1_recv[1, q].astype(F32)
        fin[pl.ds(out_chunk(q) * CH * nvec, CH * nvec), :] = total.reshape(CH * nvec, PATCH)

    def at(i, offset, limit, step):
        @pl.when((i >= offset) & (i < offset + limit))
        def _():
            step(i - offset)

    @pl.loop(0, 17)
    def _(i):
        at(i, 13, 4, scatter_last)
        at(i, 12, 4, scatter_second)
        at(i, 11, 4, scatter_first)
        for step in (3, 2, 1):
            at(i, 5 + step, count, lambda p, step=step: gather_step(step, p))
        at(i, 5, count, gather_first)
        at(i, 4, count, reduce_last)
        for step in (3, 2, 1):
            at(i, step, count, lambda p, step=step: reduce_step(step, p))
        at(i, 0, count, forward)
        at(i, 9, count, gather_last)
        at(i, 10, 4, backward)

    for n in range(nvec):
        fb[pl.ds(n, PATCH, stride=nvec), :] = fin[pl.ds(n, half, stride=nvec), :].T
    out_ref[...] = fb[...].reshape(PATCH, nvec, half).astype(BF16)

    for which in range(2):
        o_copy(which).wait_send()

    @pl.loop(0, count)
    def _(p):
        y_copy(p).wait_send()
        for way in range(2):
            for step in range(4):
                rs_copy(way, step, p).wait_send()
                ag_copy(way, step, p).wait_send()

    @pl.loop(0, 4)
    def _(q):
        core_copy(q).wait_send()
        for way in range(2):
            x0_copy(way, q).wait_send()
            x1_copy(way, q).wait_send()


def per_device(sources, transfer_matrix, delay_groups, patch_block):
    panel_dev, nvec, half = sources.shape
    mic_dev = transfer_matrix.shape[0]
    patches, blocks = delay_groups.shape
    vm = pltpu.VMEM
    dma = pltpu.SemaphoreType.DMA
    scratch = [
        vm((panel_dev, nvec, half), BF16),
        vm((mic_dev, panel_dev), BF16),
        vm((PATCH * nvec, half), F32),
        vm((half * nvec, PATCH), F32),
        vm((half + 2 * CH, nvec, panel_dev), BF16),
        vm((5, NZ, ROWS, nvec, mic_dev), BF16),
        vm((2, 4, 5, ROWS, nvec, mic_dev), BF16),
        vm((2, 3, 5, ROWS, nvec, mic_dev), BF16),
        vm((5, ROWS, nvec, mic_dev), BF16),
        vm((5, ROWS, nvec, mic_dev), BF16),
        vm((2, ROWS, nvec, mic_dev), BF16),
        vm((5, NZ, ROWS, nvec, mic_dev), BF16),
        vm((half + CH, nvec, mic_dev), BF16),
        vm((4, NX, CH, nvec, PATCH), BF16),
        vm((4, NX, CH, nvec, PATCH), BF16),
        vm((4, NX, CH, nvec, PATCH), BF16),
        vm((2, 4, CH // 2, nvec, PATCH), BF16),
        vm((2, 4, CH // 2, nvec, PATCH), BF16),
        vm((2, 4, CH, nvec, PATCH), BF16),
        vm((2, 4, CH, nvec, PATCH), BF16),
        vm((half * nvec, PATCH), F32),
        dma((patches + 1,)),
        dma((2, 4, 5)), dma((2, 4, 5)),
        dma((5,)), dma((5,)),
        dma((2,)), dma((2,)),
        dma((2, 4, 5)), dma((2, 4, 5)),
        dma((4,)), dma((4,)),
        dma((2, 4)), dma((2, 4)),
        dma((2, 4)), dma((2, 4)),
    ]
    delays, tiles = pl.pallas_call(
        reorder,
        out_shape=(
            jax.ShapeDtypeStruct((patches * blocks,), jnp.int32),
            jax.ShapeDtypeStruct((mic_dev, panel_dev), BF16),
        ),
        in_specs=[pl.BlockSpec(memory_space=pltpu.SMEM)] * 2 + [pl.BlockSpec(memory_space=pltpu.VMEM)],
        out_specs=(pl.BlockSpec(memory_space=pltpu.SMEM), pl.BlockSpec(memory_space=pltpu.VMEM)),
    )(delay_groups, patch_block, transfer_matrix)
    return pl.pallas_call(
        body,
        out_shape=jax.ShapeDtypeStruct((PATCH, nvec, half), BF16),
        in_specs=[pl.BlockSpec(memory_space=pltpu.SMEM)] + [pl.BlockSpec(memory_space=pl.ANY)] * 2,
        out_specs=pl.BlockSpec(memory_space=pltpu.VMEM),
        scratch_shapes=scratch,
        compiler_params=pltpu.CompilerParams(
            collective_id=0, has_side_effects=True, vmem_limit_bytes=56 * 1024 * 1024
        ),
    )(delays, sources, tiles)


def solution(mesh):
    placed = (P("panel", None, "tm"), P("mic", "panel"), P("panel", "mic"), P("panel"))
    return jax.shard_map(
        per_device,
        mesh=mesh,
        in_specs=placed,
        out_specs=P(("panel", "mic"), None, "tm"),
        check_vma=False,
    )
```

time: 274 us -> 79.1 us (0.29)
  blocking collectives: 111 us -> 0 us
  Pallas kernels: 0 us -> 75.3 us
  local copies, waits for them, and re-layouts: 60.1 us -> 3.02 us
  waiting for transfers between devices: 48.8 us -> 0 us
  matrix products: 27.9 us -> 0 us
  between operations: 13.6 us -> 0.02 us
  other arithmetic: 7.58 us -> 0 us
  starting transfers between devices: 4.68 us -> 0 us
    psum x1 -> x0, blocking collectives: 111 us -> none  [per_device(): pressure = lax.psum(partial_value, 'panel').astype(jnp.bfloat16)]
    pallas_call x0 -> x2, Pallas kernels: none -> 75.3 us  [the longest x1 72.8 us: per_device(): pl.pallas_call(body, out_shape=jax.ShapeDtypeStruct((PATCH, nvec, half),...]
    reduce_scatter x1 -> x0, waiting for transfers between devices: 35.5 us -> none  [per_device(): lax.psum_scatter(accum.reshape(row_count, nvec, half).astype(jnp.bfloat16...]
    dot_general x8 -> x0, matrix products: 27.9 us -> none  [the longest x4 17.4 us: per_device(): jnp.einsum('mqp,qmnt->qpnt', block_tiles, advanced, preferred_element_typ...]
    gather x13 -> x0, local copies, waits for them, and re-layouts: 23 us -> none  [the longest x4 10.2 us: one_slab(): return lax.dynamic_slice_in_dim(single_slab, offset_value, length, axis=2)]
    reshape x6 -> x0, local copies, waits for them, and re-layouts: 22.8 us -> none  [the longest x4 15.3 us: per_device(): shifted = shifted.reshape(panel_dev, nvec, half)]
    ppermute x2 -> x0, waiting for transfers between devices: 13.3 us -> none  [from_behind(): lax.ppermute(value, axis, [(source, source + steps) for source in range(i...]
    concatenate x4 -> x0, other arithmetic: 7.11 us -> none  [the longest x1 5.23 us: per_device(): extended = jnp.concatenate([rim, sources], axis=2)]
  transfers between devices with their start and end apart: 3 -> 0, of which waited for: 3 -> 0; matrix products, arithmetic and copies ran while one was open for 2% -> 0% of each run, Pallas kernels for 0% -> 0%
where the time goes in v1:
time: 79.1 us; the launch traced here: 78.4 us
  Pallas kernels  75.3 us (95%)
  local copies, waits for them, and re-layouts  3.02 us (4%)
    pallas_call x1, Pallas kernels, per_device(): pl.pallas_call(body, out_shape=jax.ShapeDtypeStruct((PATCH, nvec, half),...  72.8 us
    unnamed x2, local copies, waits for them, and re-layouts  3.02 us
    pallas_call x1, Pallas kernels, per_device(): pl.pallas_call(reorder, out_shape=(jax.ShapeDtypeStruct((patches * blocks...  2.53 us

profile of v1, /device:TPU:16, one launch (start us, length us, event | category | flops | bytes accessed | tf_op | source)
XLA Modules:
  0.0 78.4 jit_solution(5209410455297410601)
XLA Ops:
  0.0 1.3 %copy.5.dg_ref = s32[8,4]{1,0:T(8,128)} copy(s32[8,4]{0,1:T(4,128)} %param.6) | data formatting | bytes 256 | tf_op args[2]
  1.3 2.5 %shard_map.46 = (s32[32]{0:T(128)}, bf16[512,1024]{1,0:T(8,128)(2,1)}) custom-call(s32[8,4]{1,0:T(8,128)} %copy.5.dg_ref, s32[8]{0:T(128)} %pb_ref.1, bf16[512,1024]{1,0:T(8,128)(2,1)} %mat.1), custom_call_target="tpu_custom_call" | custom-call | tf_op jit(solution)/shard_map/pallas_call | solution.py:360
  3.9 72.8 %shard_map.47 = bf16[128,8,128]{2,1,0:T(8,128)(2,1)} custom-call(s32[32]{0:T(128)} %get-tuple-element.7.delays, bf16[1024,8,128]{2,1,0:T(8,128)(2,1)} %src_hbm.1, bf16[512,1024]{1,0:T(8,128)(2,1)} %get-tuple-element.8.mat_hbm), custom_call_target="tpu_custom_call" | custom-call | tf_op jit(solution)/shard_map/pallas_call | solution.py:369
  76.7 1.7 %copy.7 = bf16[128,8,128]{2,1,0:T(8,128)(2,1)} copy(bf16[128,8,128]{2,1,0:T(8,128)(2,1)} %shard_map.47) | data formatting | bytes 524288

commit v2 on v0

v2 whole, which is shorter than its diff:
```python
import jax
import jax.numpy as jnp
from jax import lax
from jax.experimental import pallas as pl
from jax.experimental.pallas import tpu as pltpu
from jax.sharding import PartitionSpec as P

DMAX = 32
PATCH = 128
MB = 128
NVEC = 8
NZ = 8
NX = 4
NCH = 8
CH = 16
ROWS = CH // NZ
OVER = DMAX // CH
MESH = pl.DeviceIdType.MESH
F32 = jnp.float32
BF16 = jnp.bfloat16
ORDER = (
    ("v", 0), ("f", 0), ("s", 0), ("s", 1), ("f", 1), ("s", 2), ("s", 3), ("f", 2), ("s", 4), ("s", 5),
    ("f", 3), ("t", 0), ("t", 1), ("t", 2), ("t", 3), ("m", 0), ("s", 6), ("s", 7), ("t", 4), ("t", 5),
    ("o", 0), ("o", 1), ("o", 2), ("o", 3), ("t", 6), ("t", 7), ("g", 0), ("g", 1), ("o", 4), ("g", 2),
    ("o", 5), ("g", 3), ("o", 6), ("o", 7), ("h", 0), ("g", 4), ("g", 5), ("h", 1), ("h", 2), ("g", 6),
    ("h", 3), ("g", 7), ("w", 0), ("h", 4), ("h", 5), ("w", 1), ("w", 2), ("b", 0), ("d", 0), ("h", 6),
    ("w", 3), ("b", 1), ("d", 1), ("h", 7), ("x", 0), ("w", 4), ("b", 2), ("d", 2), ("w", 5), ("b", 3),
    ("x", 1), ("d", 3), ("w", 6), ("b", 4), ("d", 4), ("x", 2), ("w", 7), ("b", 5), ("d", 5), ("e", 0),
    ("x", 3), ("e", 1), ("x", 4), ("k", 0), ("x", 5), ("b", 6), ("b", 7), ("d", 6), ("d", 7), ("e", 2),
    ("e", 3), ("e", 4), ("x", 6), ("x", 7), ("e", 5), ("e", 6), ("e", 7),
)


def reorder(dg_ref, pb_ref, mat, delays, tiles):
    patches, blocks = dg_ref.shape
    base = lax.axis_index("panel") * patches
    for j in range(patches):
        owner = jnp.int32(0)
        for q in range(patches):
            owner = owner + jnp.where(pb_ref[q] - base == j, q, 0)
        for b in range(blocks):
            delays[j * blocks + b] = dg_ref[owner, b]
        cols = pl.ds(pl.multiple_of(owner * PATCH, PATCH), PATCH)
        tiles[:, j * PATCH : (j + 1) * PATCH] = mat[:, cols]


def body(
    delays, src_hbm, mat_hbm, out_ref,
    sbuf, tiles, fa, fb, st, part, o_part, o_recv, r_half, r_recv, r_send, y_send, y_recv, gath, o_gath, work,
    g_send, g_keep, g_recv, x_send, x_recv, fin,
    in_sem, r_ss, r_rs, y_ss, y_rs, o_ss, o_rs, a_ss, a_rs, b_ss, b_rs, c_ss, c_rs, x_ss, x_rs,
):
    panel_dev, nvec, half = sbuf.shape
    patches = panel_dev // PATCH
    blocks = tiles.shape[0] // MB
    panel, mic, tm = (lax.axis_index(name) for name in ("panel", "mic", "tm"))
    z, y_hi = panel // 2, panel % 2
    x, core = mic // 2, mic % 2

    def z_at(step):
        return (z + step + NZ) % NZ

    def x_at(step):
        return (x + step + NX) % NX

    def z_peer(step):
        return {"panel": z_at(step) * 2 + y_hi}

    def x_peer(step):
        return {"mic": x_at(step) * 2 + core}

    y_peer = {"panel": z * 2 + 1 - y_hi}
    t_peer = {"tm": 1 - tm}
    core_peer = {"mic": x * 2 + 1 - core}
    signs = (1, -1)
    hops = (1, -1, 2)

    barrier = pltpu.get_barrier_semaphore()
    peers = [z_peer(k) for k in (1, -1, 2, -2)] + [y_peer, t_peer, core_peer] + [x_peer(k) for k in hops]
    for peer in peers:
        pl.semaphore_signal(barrier, inc=1, device_id=peer, device_id_type=MESH)

    def load_src(j):
        return pltpu.make_async_copy(
            src_hbm.at[pl.ds(j * PATCH, PATCH)], sbuf.at[pl.ds(j * PATCH, PATCH)], in_sem.at[j]
        )

    load_mat = pltpu.make_async_copy(mat_hbm, tiles, in_sem.at[patches])
    for j in range(patches):
        load_src(j).start()
    load_mat.start()

    st[0:DMAX] = jnp.zeros((DMAX,) + st.shape[1:], st.dtype)
    st[half + DMAX : half + 2 * DMAX] = jnp.zeros((DMAX,) + st.shape[1:], st.dtype)
    work[half : half + DMAX] = jnp.zeros((DMAX,) + work.shape[1:], work.dtype)

    @pl.loop(0, patches)
    def _(j):
        load_src(j).wait()
        fa[...] = sbuf[pl.ds(j * PATCH, PATCH)].astype(F32).reshape(PATCH * nvec, half)
        for n in range(nvec):
            fb[pl.ds(n, half, stride=nvec), :] = fa[pl.ds(n, PATCH, stride=nvec), :].T
        st[DMAX : DMAX + half, :, pl.ds(pl.multiple_of(j * PATCH, PATCH), PATCH)] = (
            fb[...].reshape(half, nvec, PATCH).astype(st.dtype)
        )

    load_mat.wait()
    pl.semaphore_wait(barrier, len(peers))

    def send(source, target, send_sem, recv_sem, peer):
        return pltpu.make_async_remote_copy(
            src_ref=source, dst_ref=target, send_sem=send_sem, recv_sem=recv_sem, device_id=peer, device_id_type=MESH
        )

    def chunk(p):
        return NCH - 1 - p

    def r_copy(kind, way, p):
        sign, c = signs[way], chunk(p)
        sems = r_ss.at[kind, way, p], r_rs.at[kind, way, p]
        if kind == 0:
            return send(part.at[c, z_at(4), pl.ds(way, 1)], r_half.at[way, p], *sems, z_peer(2 * sign))
        if kind == 3:
            return send(r_send.at[way, p], r_recv.at[2, way, p], *sems, z_peer(2 * sign))
        source = part.at[c, z_at(3 * sign if kind == 1 else sign)]
        return send(source, r_recv.at[kind - 1, way, p], *sems, z_peer(sign))

    def y_copy(p):
        return send(y_send.at[p], y_recv.at[p], y_ss.at[p], y_rs.at[p], y_peer)

    def a_copy(kind, way, p):
        sign = signs[way]
        ref = gath.at[p, z] if kind < 2 else gath.at[p, z_at(-2 * sign)]
        if kind == 3:
            ref = gath.at[p, z_at(-2 * sign), pl.ds(way, 1)]
        return send(ref, ref, a_ss.at[kind, way, p], a_rs.at[kind, way, p], z_peer(sign if kind in (0, 2) else 2 * sign))

    def b_copy(step, p):
        k = p - (NCH - OVER)
        return send(
            gath.at[p, z_at(step)], o_gath.at[k, z_at(step)], b_ss.at[step + 3, k], b_rs.at[step + 3, k], t_peer
        )

    def b_start(p, steps):
        if p >= NCH - OVER:

            @pl.when(tm == 1)
            def _():
                for step in steps:
                    b_copy(step, p).start()

    o_copy = send(o_part, o_recv, o_ss, o_rs, t_peer)

    def core_copy(q):
        return send(g_send.at[q], g_recv.at[q], c_ss.at[q], c_rs.at[q], core_peer)

    def x_copy(k, q):
        return send(x_send.at[k, q], x_recv.at[k, q], x_ss.at[k, q], x_rs.at[k, q], x_peer(hops[k]))

    def pressures(first, rows, put):
        for b in range(blocks):
            pieces = []
            for j in range(patches):
                at = pl.ds(first + DMAX - delays[j * blocks + b], rows)
                pieces.append(st[at, :, j * PATCH : (j + 1) * PATCH].reshape(rows * nvec, PATCH))
            acc = lax.dot_general(
                jnp.concatenate(pieces, axis=1), tiles[b * MB : (b + 1) * MB, :],
                (((1,), (1,)), ((), ())), preferred_element_type=F32,
            )
            put(b, acc.astype(BF16))

    def overlap(_):
        @pl.when(tm == 0)
        def _():
            def put(b, value):
                o_part[:, :, b * MB : (b + 1) * MB] = value.reshape(DMAX, nvec, MB)

            pressures(half, DMAX, put)
            o_copy.start()

    def forward(i):
        c = NCH - 2 - 2 * i

        def put(b, value):
            part[c : c + 2, :, :, :, b * MB : (b + 1) * MB] = value.reshape(2, NZ, ROWS, nvec, MB)

        pressures(c * CH, 2 * CH, put)

    def add_overlap(_):
        @pl.when(tm == 1)
        def _():
            o_copy.wait_recv()
            part[0:OVER] = (
                part[0:OVER].astype(F32) + o_recv[...].reshape(OVER, NZ, ROWS, nvec, blocks * MB).astype(F32)
            ).astype(BF16)

    def reduce_first(p):
        for kind in range(3):
            for way in range(2):
                r_copy(kind, way, p).start()

    def reduce_second(p):
        for way in range(2):
            r_copy(0, way, p).wait_recv()
            r_copy(1, way, p).wait_recv()
            dest = z_at(2 * signs[way])
            total = part[chunk(p), dest].astype(F32) + r_recv[0, way, p].astype(F32)
            r_send[way, p, 1 - way] = total[1 - way].astype(BF16)
            r_send[way, p, way] = (total[way] + r_half[way, p, 0].astype(F32)).astype(BF16)
            r_copy(3, way, p).start()

    def own_sum(p):
        total = part[chunk(p), z].astype(F32)
        for kind in (1, 2):
            for way in range(2):
                total = total + r_recv[kind, way, p].astype(F32)
        return total

    def reduce_last(p):
        for way in range(2):
            r_copy(2, way, p).wait_recv()
            r_copy(3, way, p).wait_recv()
        y_send[p] = own_sum(p).astype(BF16)
        y_copy(p).start()

    def gather_first(p):
        y_copy(p).wait_recv()
        gath[p, z] = (own_sum(p) + y_recv[p].astype(F32)).astype(BF16)
        for kind in (1, 0):
            for way in range(2):
                a_copy(kind, way, p).start()
        b_start(p, (0,))

    def gather_second(p):
        for way in range(2):
            a_copy(1, way, p).wait_recv()
            for kind in (3, 2):
                a_copy(kind, way, p).start()
        for way in range(2):
            a_copy(0, way, p).wait_recv()
        b_start(p, (1, -1, 2, -2))

    def gather_last(p):
        for way in range(2):
            a_copy(2, way, p).wait_recv()
            a_copy(3, way, p).wait_recv()
        b_start(p, (3, -3, 4))
        c = chunk(p)
        work[c * CH : (c + 1) * CH] = gath[p].reshape(CH, nvec, blocks * MB)

    def take_overlap(_):
        @pl.when(tm == 0)
        def _():
            for p in range(NCH - OVER, NCH):
                for step in range(-3, 5):
                    b_copy(step, p).wait_recv()
                first = half + chunk(p) * CH
                work[first : first + CH] = o_gath[p - (NCH - OVER)].reshape(CH, nvec, blocks * MB)

    def out_chunk(q):
        return jnp.where(tm == 0, (NCH - 1 - OVER - q) % NCH, NCH - 1 - q)

    def products(q, target, side):
        start = out_chunk(q) * CH
        for k in range(NX):
            j = 2 * k + side
            pieces = []
            for b in range(blocks):
                at = pl.ds(start + delays[j * blocks + b], CH)
                pieces.append(work[at, :, b * MB : (b + 1) * MB].reshape(CH * nvec, MB))
            acc = jnp.dot(
                jnp.concatenate(pieces, axis=1), tiles[:, pl.ds(pl.multiple_of(j * PATCH, PATCH), PATCH)],
                preferred_element_type=F32,
            )
            target[q, k] = acc.reshape(CH, nvec, PATCH).astype(BF16)

    def backward_away(q):
        products(q, g_send, 1 - core)
        core_copy(q).start()

    def backward_own(q):
        products(q, g_keep, core)

    def pair(q, dest):
        return g_keep[q, dest].astype(F32) + g_recv[q, dest].astype(F32)

    def scatter(q):
        core_copy(q).wait_recv()
        for k in (2, 0, 1):
            x_send[k, q] = pair(q, x_at(hops[k])).astype(BF16)
            x_copy(k, q).start()

    def scatter_last(q):
        total = pair(q, x)
        for k in range(3):
            x_copy(k, q).wait_recv()
            total = total + x_recv[k, q].astype(F32)
        fin[pl.ds(out_chunk(q) * CH * nvec, CH * nvec), :] = total.reshape(CH * nvec, PATCH)

    steps = {
        "v": overlap, "f": forward, "m": add_overlap, "s": reduce_first, "t": reduce_second, "o": reduce_last,
        "g": gather_first, "h": gather_second, "w": gather_last, "k": take_overlap,
        "b": backward_away, "d": backward_own, "x": scatter, "e": scatter_last,
    }
    for letter, place in ORDER:
        steps[letter](place)

    for n in range(nvec):
        fb[pl.ds(n, PATCH, stride=nvec), :] = fin[pl.ds(n, half, stride=nvec), :].T
    out_ref[...] = fb[...].reshape(PATCH, nvec, half).astype(BF16)

    @pl.when(tm == 0)
    def _():
        o_copy.wait_send()

    @pl.when(tm == 1)
    def _():
        for p in range(NCH - OVER, NCH):
            for step in range(-3, 5):
                b_copy(step, p).wait_send()

    for p in range(NCH):
        y_copy(p).wait_send()
        core_copy(p).wait_send()
        for k in range(3):
            x_copy(k, p).wait_send()
        for kind in range(4):
            for way in range(2):
                r_copy(kind, way, p).wait_send()
                a_copy(kind, way, p).wait_send()


def per_device(sources, transfer_matrix, delay_groups, patch_block):
    panel_dev, nvec, half = sources.shape
    mic_dev = transfer_matrix.shape[0]
    patches, blocks = delay_groups.shape
    vm = pltpu.VMEM
    dma = pltpu.SemaphoreType.DMA
    own = (ROWS, nvec, mic_dev)
    scratch = [
        vm((panel_dev, nvec, half), BF16),
        vm((mic_dev, panel_dev), BF16),
        vm((PATCH * nvec, half), F32),
        vm((half * nvec, PATCH), F32),
        vm((half + 2 * DMAX, nvec, panel_dev), BF16),
        vm((NCH, NZ) + own, BF16),
        vm((DMAX, nvec, mic_dev), BF16),
        vm((DMAX, nvec, mic_dev), BF16),
        vm((2, NCH, 1, nvec, mic_dev), BF16),
        vm((3, 2, NCH) + own, BF16),
        vm((2, NCH) + own, BF16),
        vm((NCH,) + own, BF16),
        vm((NCH,) + own, BF16),
        vm((NCH, NZ) + own, BF16),
        vm((OVER, NZ) + own, BF16),
        vm((half + DMAX, nvec, mic_dev), BF16),
        vm((NCH, NX, CH, nvec, PATCH), BF16),
        vm((NCH, NX, CH, nvec, PATCH), BF16),
        vm((NCH, NX, CH, nvec, PATCH), BF16),
        vm((3, NCH, CH, nvec, PATCH), BF16),
        vm((3, NCH, CH, nvec, PATCH), BF16),
        vm((half * nvec, PATCH), F32),
        dma((patches + 1,)),
        dma((4, 2, NCH)), dma((4, 2, NCH)),
        dma((NCH,)), dma((NCH,)),
        dma, dma,
        dma((4, 2, NCH)), dma((4, 2, NCH)),
        dma((NZ, OVER)), dma((NZ, OVER)),
        dma((NCH,)), dma((NCH,)),
        dma((3, NCH)), dma((3, NCH)),
    ]
    delays, tiles = pl.pallas_call(
        reorder,
        out_shape=(
            jax.ShapeDtypeStruct((patches * blocks,), jnp.int32),
            jax.ShapeDtypeStruct((mic_dev, panel_dev), BF16),
        ),
        in_specs=[pl.BlockSpec(memory_space=pltpu.SMEM)] * 2 + [pl.BlockSpec(memory_space=pltpu.VMEM)],
        out_specs=(pl.BlockSpec(memory_space=pltpu.SMEM), pl.BlockSpec(memory_space=pltpu.VMEM)),
    )(delay_groups, patch_block, transfer_matrix)
    return pl.pallas_call(
        body,
        out_shape=jax.ShapeDtypeStruct((PATCH, nvec, half), BF16),
        in_specs=[pl.BlockSpec(memory_space=pltpu.SMEM)] + [pl.BlockSpec(memory_space=pl.ANY)] * 2,
        out_specs=pl.BlockSpec(memory_space=pltpu.VMEM),
        scratch_shapes=scratch,
        compiler_params=pltpu.CompilerParams(
            collective_id=0, has_side_effects=True, vmem_limit_bytes=56 * 1024 * 1024
        ),
    )(delays, sources, tiles)


def solution(mesh):
    placed = (P("panel", None, "tm"), P("mic", "panel"), P("panel", "mic"), P("panel"))
    return jax.shard_map(
        per_device,
        mesh=mesh,
        in_specs=placed,
        out_specs=P(("panel", "mic"), None, "tm"),
        check_vma=False,
    )
```

time: 274 us -> 64.6 us (0.24)
  blocking collectives: 111 us -> 0 us
  Pallas kernels: 0 us -> 61.4 us
  local copies, waits for them, and re-layouts: 60.1 us -> 3.02 us
  waiting for transfers between devices: 48.8 us -> 0 us
  matrix products: 27.9 us -> 0 us
  between operations: 13.6 us -> 0.02 us
  other arithmetic: 7.58 us -> 0 us
  starting transfers between devices: 4.68 us -> 0 us
    psum x1 -> x0, blocking collectives: 111 us -> none  [per_device(): pressure = lax.psum(partial_value, 'panel').astype(jnp.bfloat16)]
    pallas_call x0 -> x2, Pallas kernels: none -> 61.4 us  [the longest x1 58.9 us: per_device(): pl.pallas_call(body, out_shape=jax.ShapeDtypeStruct((PATCH, nvec, half),...]
    reduce_scatter x1 -> x0, waiting for transfers between devices: 35.5 us -> none  [per_device(): lax.psum_scatter(accum.reshape(row_count, nvec, half).astype(jnp.bfloat16...]
    dot_general x8 -> x0, matrix products: 27.9 us -> none  [the longest x4 17.4 us: per_device(): jnp.einsum('mqp,qmnt->qpnt', block_tiles, advanced, preferred_element_typ...]
    gather x13 -> x0, local copies, waits for them, and re-layouts: 23 us -> none  [the longest x4 10.2 us: one_slab(): return lax.dynamic_slice_in_dim(single_slab, offset_value, length, axis=2)]
    reshape x6 -> x0, local copies, waits for them, and re-layouts: 22.8 us -> none  [the longest x4 15.3 us: per_device(): shifted = shifted.reshape(panel_dev, nvec, half)]
    ppermute x2 -> x0, waiting for transfers between devices: 13.3 us -> none  [from_behind(): lax.ppermute(value, axis, [(source, source + steps) for source in range(i...]
    concatenate x4 -> x0, other arithmetic: 7.11 us -> none  [the longest x1 5.23 us: per_device(): extended = jnp.concatenate([rim, sources], axis=2)]
  transfers between devices with their start and end apart: 3 -> 0, of which waited for: 3 -> 0; matrix products, arithmetic and copies ran while one was open for 2% -> 0% of each run, Pallas kernels for 0% -> 0%
where the time goes in v2:
time: 64.6 us; the launch traced here: 64.4 us
  Pallas kernels  61.4 us (95%)
  local copies, waits for them, and re-layouts  3.02 us (5%)
    pallas_call x1, Pallas kernels, per_device(): pl.pallas_call(body, out_shape=jax.ShapeDtypeStruct((PATCH, nvec, half),...  58.9 us
    unnamed x2, local copies, waits for them, and re-layouts  3.02 us
    pallas_call x1, Pallas kernels, per_device(): pl.pallas_call(reorder, out_shape=(jax.ShapeDtypeStruct((patches * blocks...  2.53 us

profile of v2, /device:TPU:16, one launch (start us, length us, event | category | flops | bytes accessed | tf_op | source)
XLA Modules:
  0.0 64.4 jit_solution(17742762490445776414)
XLA Ops:
  0.0 1.3 %copy.5.dg_ref = s32[8,4]{1,0:T(8,128)} copy(s32[8,4]{0,1:T(4,128)} %param.6) | data formatting | bytes 256 | tf_op args[2]
  1.3 2.5 %shard_map.46 = (s32[32]{0:T(128)}, bf16[512,1024]{1,0:T(8,128)(2,1)}) custom-call(s32[8,4]{1,0:T(8,128)} %copy.5.dg_ref, s32[8]{0:T(128)} %pb_ref.1, bf16[512,1024]{1,0:T(8,128)(2,1)} %mat.1), custom_call_target="tpu_custom_call" | custom-call | tf_op jit(solution)/shard_map/pallas_call | solution.py:372
  3.9 58.9 %shard_map.47 = bf16[128,8,128]{2,1,0:T(8,128)(2,1)} custom-call(s32[32]{0:T(128)} %get-tuple-element.7.delays, bf16[1024,8,128]{2,1,0:T(8,128)(2,1)} %src_hbm.1, bf16[512,1024]{1,0:T(8,128)(2,1)} %get-tuple-element.8.mat_hbm), custom_call_target="tpu_custom_call" | custom-call | tf_op jit(solution)/shard_map/pallas_call | solution.py:381
  62.8 1.7 %copy.7 = bf16[128,8,128]{2,1,0:T(8,128)(2,1)} copy(bf16[128,8,128]{2,1,0:T(8,128)(2,1)} %shard_map.47) | data formatting | bytes 524288

commit v3 on v2

--- a/solution.py
+++ b/solution.py
@@ -31,23 +31,10 @@
 )
 
 
-def reorder(dg_ref, pb_ref, mat, delays, tiles):
-    patches, blocks = dg_ref.shape
-    base = lax.axis_index("panel") * patches
-    for j in range(patches):
-        owner = jnp.int32(0)
-        for q in range(patches):
-            owner = owner + jnp.where(pb_ref[q] - base == j, q, 0)
-        for b in range(blocks):
-            delays[j * blocks + b] = dg_ref[owner, b]
-        cols = pl.ds(pl.multiple_of(owner * PATCH, PATCH), PATCH)
-        tiles[:, j * PATCH : (j + 1) * PATCH] = mat[:, cols]
-
-
 def body(
-    delays, src_hbm, mat_hbm, out_ref,
-    sbuf, tiles, fa, fb, st, part, o_part, o_recv, r_half, r_recv, r_send, y_send, y_recv, gath, o_gath, work,
-    g_send, g_keep, g_recv, x_send, x_recv, fin,
+    dg_ref, pb_ref, src_hbm, mat_hbm, out_ref,
+    sbuf, mat, tiles, fa, fb, st, part, o_part, o_recv, r_half, r_recv, r_send, y_send, y_recv, gath, o_gath, work,
+    g_send, g_keep, g_recv, x_send, x_recv, fin, delays,
     in_sem, r_ss, r_rs, y_ss, y_rs, o_ss, o_rs, a_ss, a_rs, b_ss, b_rs, c_ss, c_rs, x_ss, x_rs,
 ):
     panel_dev, nvec, half = sbuf.shape
@@ -85,10 +72,21 @@
             src_hbm.at[pl.ds(j * PATCH, PATCH)], sbuf.at[pl.ds(j * PATCH, PATCH)], in_sem.at[j]
         )
 
-    load_mat = pltpu.make_async_copy(mat_hbm, tiles, in_sem.at[patches])
+    load_mat = pltpu.make_async_copy(mat_hbm, mat, in_sem.at[patches])
     for j in range(patches):
         load_src(j).start()
     load_mat.start()
+
+    names = []
+    for j in range(patches):
+        apart = [pb_ref[q] - panel * patches - j for q in range(patches)]
+        names.append([1 - jnp.minimum(gap * gap, 1) for gap in apart])
+    for j in range(patches):
+        for b in range(blocks):
+            total = names[j][0] * dg_ref[b, 0]
+            for q in range(1, patches):
+                total = total + names[j][q] * dg_ref[b, q]
+            delays[j * blocks + b] = total
 
     st[0:DMAX] = jnp.zeros((DMAX,) + st.shape[1:], st.dtype)
     st[half + DMAX : half + 2 * DMAX] = jnp.zeros((DMAX,) + st.shape[1:], st.dtype)
@@ -105,6 +103,17 @@
         )
 
     load_mat.wait()
+    for j in range(patches):
+        weights = [names[j][q].astype(F32) for q in range(patches)]
+
+        @pl.loop(0, mat.shape[0] // 64)
+        def _(i):
+            rows = pl.ds(pl.multiple_of(i * 64, 64), 64)
+            total = weights[0] * mat[rows, 0:PATCH].astype(F32)
+            for q in range(1, patches):
+                total = total + weights[q] * mat[rows, q * PATCH : (q + 1) * PATCH].astype(F32)
+            tiles[rows, j * PATCH : (j + 1) * PATCH] = total.astype(BF16)
+
     pl.semaphore_wait(barrier, len(peers))
 
     def send(source, target, send_sem, recv_sem, peer):
@@ -339,6 +348,7 @@
     own = (ROWS, nvec, mic_dev)
     scratch = [
         vm((panel_dev, nvec, half), BF16),
+        vm((mic_dev, panel_dev), BF16),
         vm((mic_dev, panel_dev), BF16),
         vm((PATCH * nvec, half), F32),
         vm((half * nvec, PATCH), F32),
@@ -360,6 +370,7 @@
         vm((3, NCH, CH, nvec, PATCH), BF16),
         vm((3, NCH, CH, nvec, PATCH), BF16),
         vm((half * nvec, PATCH), F32),
+        pltpu.SMEM((patches * blocks,), jnp.int32),
         dma((patches + 1,)),
         dma((4, 2, NCH)), dma((4, 2, NCH)),
         dma((NCH,)), dma((NCH,)),
@@ -369,25 +380,16 @@
         dma((NCH,)), dma((NCH,)),
         dma((3, NCH)), dma((3, NCH)),
     ]
-    delays, tiles = pl.pallas_call(
-        reorder,
-        out_shape=(
-            jax.ShapeDtypeStruct((patches * blocks,), jnp.int32),
-            jax.ShapeDtypeStruct((mic_dev, panel_dev), BF16),
-        ),
-        in_specs=[pl.BlockSpec(memory_space=pltpu.SMEM)] * 2 + [pl.BlockSpec(memory_space=pltpu.VMEM)],
-        out_specs=(pl.BlockSpec(memory_space=pltpu.SMEM), pl.BlockSpec(memory_space=pltpu.VMEM)),
-    )(delay_groups, patch_block, transfer_matrix)
     return pl.pallas_call(
         body,
         out_shape=jax.ShapeDtypeStruct((PATCH, nvec, half), BF16),
-        in_specs=[pl.BlockSpec(memory_space=pltpu.SMEM)] + [pl.BlockSpec(memory_space=pl.ANY)] * 2,
+        in_specs=[pl.BlockSpec(memory_space=pltpu.SMEM)] * 2 + [pl.BlockSpec(memory_space=pl.ANY)] * 2,
         out_specs=pl.BlockSpec(memory_space=pltpu.VMEM),
         scratch_shapes=scratch,
         compiler_params=pltpu.CompilerParams(
             collective_id=0, has_side_effects=True, vmem_limit_bytes=56 * 1024 * 1024
         ),
-    )(delays, sources, tiles)
+    )(delay_groups.T, patch_block, sources, transfer_matrix)
 
 
 def solution(mesh):

time: 64.6 us -> 62.8 us (0.972)
  local copies, waits for them, and re-layouts: 3.02 us -> 1.67 us
    pallas_call x1 -> x0, Pallas kernels: 2.53 us -> none  [per_device(): pl.pallas_call(reorder, out_shape=(jax.ShapeDtypeStruct((patches * blocks...]
    pallas_call x1, Pallas kernels: 58.9 us -> 61 us  [per_device(): pl.pallas_call(body, out_shape=jax.ShapeDtypeStruct((PATCH, nvec, half),...]
    unnamed x2 -> x1, local copies, waits for them, and re-layouts: 3.02 us -> 1.67 us
where the time goes in v3:
time: 62.8 us; the launch traced here: 62.6 us
  Pallas kernels  61 us (97%)
  local copies, waits for them, and re-layouts  1.67 us (3%)
    pallas_call x1, Pallas kernels, per_device(): pl.pallas_call(body, out_shape=jax.ShapeDtypeStruct((PATCH, nvec, half),...  61 us
    unnamed x1, local copies, waits for them, and re-layouts  1.67 us

profile of v3, /device:TPU:16, one launch (start us, length us, event | category | flops | bytes accessed | tf_op | source)
XLA Modules:
  0.0 62.6 jit_solution(17280987041868304902)
XLA Ops:
  0.0 61.0 %shard_map.46 = bf16[128,8,128]{2,1,0:T(8,128)(2,1)} custom-call(s32[4,8]{1,0:T(4,128)} %bitcast.1, s32[8]{0:T(128)} %pb_ref.1, bf16[1024,8,128]{2,1,0:T(8,128)(2,1)} %src_hbm.1, bf16[512,1024]{1,0:T(8,128)(2,1)} %mat_hbm.1), custom_call_target="tpu_custom_call" | custom-call | tf_op jit(solution)/shard_map/pallas_call | solution.py:383
  61.0 1.7 %copy.6 = bf16[128,8,128]{2,1,0:T(8,128)(2,1)} copy(bf16[128,8,128]{2,1,0:T(8,128)(2,1)} %shard_map.46) | data formatting | bytes 524288
